TPU v7x, 128 devices: a whole 4x4x4 slice. The times are simulated.
128 devices in a mesh: req: 8 (over y, core), tok: 16 (over x, z).
Axes of the slice: x: 4, y: 4, z: 4, core: 2. Of those that a mesh axis runs over, the one named last changes fastest.
Arguments:
- layer_input: bfloat16 [16384, 2048], P(('req', 'tok')), may hold values from -12 to 12
- q_in: bfloat16 [16384, 2048], P(('req', 'tok')), may hold values from -10 to 10
- k_in: bfloat16 [16384, 2048], P(('req', 'tok')), may hold values from -10 to 10
- v_in: bfloat16 [16384, 2048], P(('req', 'tok')), may hold values from -6 to 6
- segment_ids: int32 [8, 2048], P('req'), may hold values from 0 to 3, never falling along the last dimension, each value on 1 to 1024 neighbouring positions
- lambda_parts: float32 [4, 128], replicated, may hold values from -0.8 to 0.8
- out_weight: bfloat16 [2048, 2048], replicated, may hold values from -0.125 to 0.125
- ffn_gain: float32 [2048], replicated, may hold values from 0.1 to 1.9
- gate_weight: bfloat16 [2048, 5632], P(None, 'req'), may hold values from -0.125 to 0.125
- up_weight: bfloat16 [2048, 5632], P(None, 'req'), may hold values from -0.125 to 0.125
- down_weight: bfloat16 [5632, 2048], P('req'), may hold values from -0.078125 to 0.078125
- next_gain: float32 [2048], replicated, may hold values from 0.1 to 1.9
- qkv_weight: bfloat16 [2048, 6144], P(None, 'req'), may hold values from -0.125 to 0.125
- page_owner: int32 [8, 256], P('req'), may hold values from 0 to 15, as said below
- page_slot: int32 [8, 256], P('req'), may hold values from 0 to 15, as said below
Outputs:
- layer_output: bfloat16 [16384, 2048], P(('req', 'tok'))
- q_next: bfloat16 [16384, 2048], P(('req', 'tok'))
- page_cache: bfloat16 [2048, 8, 4096], P(('req', 'tok'))
Inputs may be any that keep to these rules, and one draw needn't show every extreme that they name: `segment_ids`: segment numbers never fall along a group; each of the 4 prompts of a group has 1 to 1024 tokens, one exactly 1024. `page_owner`: the 16 pages of each device name every device of its request group as owner exactly once. `page_slot`: within a request group every pair of owner and slot is named by exactly one page.
All inputs are finite; a program needn't handle non-finite values.
Results may differ from a plain program's by a relative error of at most 0.017.
Values may be sent and summed in bfloat16 or wider, within the bound.
A program may use at most 192 MiB of HBM per device.

v0:
```python
import math
import jax
import jax.numpy as jnp
from jax import lax
from jax.sharding import PartitionSpec as P

HEADS = 8
PAGE = 8
NEG_FILL = -1e30
LAMBDA_INIT = 0.2
EPSILON = 1e-05
MAX_SEG = 1024


def rms_rows(values):
    return values * lax.rsqrt(jnp.mean(values * values, axis=-1, keepdims=True) + EPSILON)


def lambda_value(lambda_parts):
    first_term = jnp.exp(jnp.sum(lambda_parts[0] * lambda_parts[1]))
    second_term = jnp.exp(jnp.sum(lambda_parts[2] * lambda_parts[3]))
    return first_term - second_term + LAMBDA_INIT


def body(
    layer_input,
    q_in,
    k_in,
    v_in,
    segment_ids,
    lambda_parts,
    out_weight,
    ffn_gain,
    gate_weight,
    up_weight,
    down_weight,
    next_gain,
    qkv_weight,
    page_owner,
    page_slot,
):
    row_count = q_in.shape[0]
    feat_width = q_in.shape[1]
    head_dim = feat_width // (2 * HEADS)
    peer_count = lax.axis_size("tok")
    tok_place = lax.axis_index("tok")
    seg_row = segment_ids[0]
    first_row = tok_place * row_count
    query_places = first_row + jnp.arange(row_count)
    query_segs = lax.dynamic_slice_in_dim(seg_row, first_row, row_count)
    lambda_mix = lambda_value(lambda_parts)
    score_scale = 1.0 / math.sqrt(head_dim)
    query_split = q_in.reshape(row_count, HEADS, 2, head_dim)
    run_max = jnp.full((HEADS, 2, row_count), NEG_FILL, jnp.float32)
    back = -(-(MAX_SEG - 1) // row_count)
    own_kv = jnp.concatenate([k_in, v_in], axis=1)
    pieces = []
    for shift in range(back, 0, -1):
        pairs = [(src_i, src_i + shift) for src_i in range(peer_count - shift)]
        pieces.append(lax.ppermute(own_kv, "tok", perm=pairs))
    pieces.append(own_kv)
    window = jnp.concatenate(pieces, axis=0)
    piece_len = window.shape[0]
    key_rows = window[:, :feat_width]
    value_rows = window[:, feat_width:]
    key_split = key_rows.reshape(piece_len, HEADS, 2, head_dim)
    value_split = value_rows.reshape(piece_len, HEADS, 2 * head_dim)
    key_places = (tok_place - back) * row_count + jnp.arange(piece_len)
    key_segs = jnp.take(seg_row, jnp.clip(key_places, 0, seg_row.shape[0] - 1))
    visible = (
        (key_places[None, :] >= 0)
        & (key_segs[None, :] == query_segs[:, None])
        & (key_places[None, :] <= query_places[:, None])
    )
    scores = (
        jnp.einsum("qhmd,khmd->hmqk", query_split, key_split, preferred_element_type=jnp.float32)
        * score_scale
    )
    scores = jnp.where(visible, scores, NEG_FILL)
    new_max = jnp.maximum(run_max, jnp.max(scores, axis=-1))
    weights = jnp.where(visible, jnp.exp(scores - new_max[..., None]), 0.0)
    totals = jnp.sum(weights, axis=-1)
    weighted = jnp.einsum(
        "hmqk,khe->hmqe",
        weights.astype(jnp.bfloat16),
        value_split,
        preferred_element_type=jnp.float32,
    )
    run_max, totals, weighted = (new_max, totals, weighted)
    map_outputs = weighted / totals[..., None]
    difference = map_outputs[:, 0] - lambda_mix * map_outputs[:, 1]
    head_outputs = rms_rows(difference) * (1.0 - LAMBDA_INIT)
    attention = (
        jnp.transpose(head_outputs, (1, 0, 2)).reshape(row_count, feat_width).astype(jnp.bfloat16)
    )
    residual_mid = (
        layer_input.astype(jnp.float32)
        + jnp.dot(attention, out_weight, preferred_element_type=jnp.float32)
    ).astype(jnp.bfloat16)
    gathered = lax.all_gather(residual_mid, "req", axis=0, tiled=True)
    normed = (rms_rows(gathered.astype(jnp.float32)) * ffn_gain).astype(jnp.bfloat16)
    gate_proj = jnp.dot(normed, gate_weight, preferred_element_type=jnp.float32)
    up_proj = jnp.dot(normed, up_weight, preferred_element_type=jnp.float32)
    hidden = (jax.nn.silu(gate_proj) * up_proj).astype(jnp.bfloat16)
    ffn_own = lax.psum_scatter(
        jnp.dot(hidden, down_weight, preferred_element_type=jnp.float32).astype(jnp.bfloat16),
        "req",
        scatter_dimension=0,
        tiled=True,
    ).astype(jnp.float32)
    layer_output = (residual_mid.astype(jnp.float32) + ffn_own).astype(jnp.bfloat16)
    next_normed = (rms_rows(layer_output.astype(jnp.float32)) * next_gain).astype(jnp.bfloat16)
    projected_cols = jnp.dot(
        lax.all_gather(next_normed, "req", axis=0, tiled=True),
        qkv_weight,
        preferred_element_type=jnp.float32,
    ).astype(jnp.bfloat16)
    projected = lax.all_to_all(projected_cols, "req", split_axis=0, concat_axis=1, tiled=True)
    q_next = projected[:, :feat_width]
    pages_dev = row_count // PAGE
    per_owner = pages_dev // peer_count
    key_values = projected[:, feat_width:].reshape(pages_dev, PAGE, 2 * feat_width)
    owner_all = page_owner[0].reshape(peer_count, pages_dev)
    slot_all = page_slot[0].reshape(peer_count, pages_dev)
    page_numbers = jnp.arange(pages_dev, dtype=jnp.int32)
    my_owners = lax.dynamic_index_in_dim(owner_all, tok_place, 0, keepdims=False)
    send_order = jnp.argsort(my_owners * pages_dev + page_numbers)
    outgoing = key_values[send_order].reshape(peer_count, per_owner, PAGE, 2 * feat_width)
    incoming = lax.all_to_all(outgoing, "tok", split_axis=0, concat_axis=0, tiled=True)
    rank_keys = jnp.where(
        owner_all == tok_place, page_numbers[None, :], pages_dev + page_numbers[None, :]
    )
    chosen_pages = jnp.argsort(rank_keys, axis=1)[:, :per_owner]
    slot_list = jnp.take_along_axis(slot_all, chosen_pages, axis=1).reshape(pages_dev)
    page_cache = (
        jnp.zeros((pages_dev, PAGE, 2 * feat_width), jnp.bfloat16)
        .at[slot_list]
        .set(incoming.reshape(pages_dev, PAGE, 2 * feat_width))
    )
    return (layer_output, q_next, page_cache)


def solution(mesh):
    in_specs = (
        P(("req", "tok"), None),
        P(("req", "tok"), None),
        P(("req", "tok"), None),
        P(("req", "tok"), None),
        P("req", None),
        P(),
        P(),
        P(),
        P(None, "req"),
        P(None, "req"),
        P("req", None),
        P(),
        P(None, "req"),
        P("req", None),
        P("req", None),
    )
    out_specs = (P(("req", "tok"), None), P(("req", "tok"), None), P(("req", "tok"), None, None))
    return jax.shard_map(body, mesh=mesh, in_specs=in_specs, out_specs=out_specs, check_vma=False)
```

profile of v0, /device:TPU:0, one launch (start us, length us, event | category | flops | bytes accessed | tf_op | source)
XLA Modules:
  0.0 437.3 jit_solution(304008285303600586)
XLA Ops:
  7.2 2.2 copy.38
  9.4 2.0 copy.39
  11.5 2.2 pad_maximum_fusion
  13.7 6.0 %collective-permute-start = (bf16[128,4096]{0,1:T(8,128)(2,1)}, bf16[128,4096]{0,1:T(8,128)(2,1)}, u32[]{:S(2)}, u32[]{:S(2)}) collective-permute-start(bf16[128,4096]{0,1:T(8,128)(2,1)} %pad_maximum_fusion), channel_id=1, source_target_pairs={{0,8},{1,9},{2,10},{3,11},{4,12},{5,13},{6,14},{7,15},{16,24},{17,... | collective-permute-start | bytes 3145736 | tf_op jit(solution)/shard_map/ppermute | solution.py:60
  19.7 7.0 %collective-permute-start.1 = (bf16[128,4096]{0,1:T(8,128)(2,1)}, bf16[128,4096]{0,1:T(8,128)(2,1)}, u32[]{:S(2)}, u32[]{:S(2)}) collective-permute-start(bf16[128,4096]{0,1:T(8,128)(2,1)} %pad_maximum_fusion), channel_id=1, source_target_pairs={{0,7},{1,8},{2,9},{3,10},{4,11},{5,12},{6,13},{7,14},{8,15},{16,23... | collective-permute-start | bytes 3145736 | tf_op jit(solution)/shard_map/ppermute | solution.py:60
  26.7 2.3 collective-permute-start.2
  29.0 2.3 collective-permute-start.3
  31.2 2.3 collective-permute-start.4
  33.6 6.5 %gather_fusion = s32[1152]{0:T(1024)S(1)} fusion(s32[2048]{0:T(1024)S(1)} %bitcast.62, s32[2048]{0:T(1024)S(1)} %pad_clamp_fusion), kind=kCustom, calls=%fused_computation | custom fusion | bytes 13824 | tf_op jit(solution)/shard_map/jit(_take)/gather | solution.py:69
  40.1 2.2 reshape.141
  42.3 1.0 compare_and_fusion
  43.4 0.7 multiply_reduce_fusion.1
  45.4 3.2 collective-permute-start.5
  48.6 2.4 constant_dynamic-update-slice_fusion.8
  51.0 14.2 %collective-permute-done.1 = bf16[128,4096]{0,1:T(8,128)(2,1)} collective-permute-done((bf16[128,4096]{0,1:T(8,128)(2,1)}, bf16[128,4096]{0,1:T(8,128)(2,1)}, u32[]{:S(2)}, u32[]{:S(2)}) %collective-permute-start.1) | collective-permute-done | bytes 1048608 | tf_op jit(solution)/shard_map/ppermute | solution.py:60
  65.1 5.8 %collective-permute-start.6 = (bf16[128,4096]{0,1:T(8,128)(2,1)}, bf16[128,4096]{0,1:T(8,128)(2,1)S(1)}, u32[]{:S(2)}, u32[]{:S(2)}) collective-permute-start(bf16[128,4096]{0,1:T(8,128)(2,1)} %pad_maximum_fusion), channel_id=1, source_target_pairs={{0,2},{1,3},{2,4},{3,5},{4,6},{5,7},{6,8},{7,9},{8,10},{9,11},{10,... | collective-permute-start | bytes 3145736 | tf_op jit(solution)/shard_map/ppermute | solution.py:60
  70.9 2.3 constant_dynamic-update-slice_fusion.7
  73.3 14.4 %collective-permute-done.2 = bf16[128,4096]{0,1:T(8,128)(2,1)} collective-permute-done((bf16[128,4096]{0,1:T(8,128)(2,1)}, bf16[128,4096]{0,1:T(8,128)(2,1)}, u32[]{:S(2)}, u32[]{:S(2)}) %collective-permute-start.2) | collective-permute-done | bytes 1048608 | tf_op jit(solution)/shard_map/ppermute | solution.py:60
  87.6 4.0 collective-permute-start.7
  91.7 2.4 constant_dynamic-update-slice_fusion.6
  94.0 16.1 %collective-permute-done.3 = bf16[128,4096]{0,1:T(8,128)(2,1)} collective-permute-done((bf16[128,4096]{0,1:T(8,128)(2,1)}, bf16[128,4096]{0,1:T(8,128)(2,1)}, u32[]{:S(2)}, u32[]{:S(2)}) %collective-permute-start.3) | collective-permute-done | bytes 1048608 | tf_op jit(solution)/shard_map/ppermute | solution.py:60
  110.1 2.4 constant_dynamic-update-slice_fusion.5
  112.5 19.0 %collective-permute-done.4 = bf16[128,4096]{0,1:T(8,128)(2,1)} collective-permute-done((bf16[128,4096]{0,1:T(8,128)(2,1)}, bf16[128,4096]{0,1:T(8,128)(2,1)}, u32[]{:S(2)}, u32[]{:S(2)}) %collective-permute-start.4) | collective-permute-done | bytes 1048608 | tf_op jit(solution)/shard_map/ppermute | solution.py:60
  131.4 2.4 constant_dynamic-update-slice_fusion.4
  133.8 1.1 constant_dynamic-update-slice_fusion.3
  135.0 1.1 constant_dynamic-update-slice_fusion.2
  136.1 1.1 constant_dynamic-update-slice_fusion.1
  137.2 1.1 constant_dynamic-update-slice_fusion
  138.3 6.8 %fusion.37 = (bf16[1152,2048]{0,1:T(8,128)(2,1)}, bf16[1152,2048]{0,1:T(8,128)(2,1)S(1)}) fusion(bf16[1152,4096]{0,1:T(8,128)(2,1)} %constant_dynamic-update-slice_fusion), kind=kLoop, calls=%fused_computation.84 | loop fusion | bytes 18874368 | tf_op jit(solution)/shard_map/slice | solution.py:65
  145.1 2.5 fusion.3
  147.6 2.3 fusion.4
  149.9 1.3 copy-done.2
  151.2 8.3 %broadcast_divide_fusion = f32[8,2,128,256]{3,2,1,0:T(8,128)S(1)} fusion(f32[8,2,128]{2,1,0:T(2,128)S(1)} %fusion.4, bf16[1152,8,256,1]{0,2,3,1:T(8,128)(2,1)} %bitcast.66, f32[8,2,1152,128]{3,2,1,0:T(8,128)} %copy-done.2, f32[8,2,128]{2,1,0:T(2,128)S(1)} %broadcast_maximum_fusion, pred[128,1152]{0,1:T(8,128)(4,1)S(1)} %compare_and_fusion), kind=kOutput, calls=%fused_computation.39 | convolution fusion | flops 1220280320 | bytes 16416768 | tf_op jit(solution)/shard_map/hmqk,khe->hmqe/dot_general | solution.py:83
  159.7 1.1 fusion.26
  160.8 2.0 copy.44
  162.9 5.7 %fusion.13 = bf16[128,2048]{1,0:T(8,128)(2,1)} fusion(bf16[128,2048]{0,1:T(8,128)(2,1)} %bitcast.68, bf16[2048,2048]{1,0:T(8,128)(2,1)} %param.21, bf16[128,2048]{1,0:T(8,128)(2,1)} %param.15), kind=kOutput, calls=%fused_computation.23 | convolution fusion | flops 1074528256 | bytes 9961472 | tf_op jit(solution)/shard_map/dot_general | solution.py:98
  168.5 0.3 reduce-scatter.2.cloned.1.call-start
  168.8 97.9 %all-gather.3.cloned.1.call-done = bf16[1024,2048]{1,0:T(8,128)(2,1)} async-done(((bf16[128,2048]{1,0:T(8,128)(2,1)}), bf16[1024,2048]{1,0:T(8,128)(2,1)}) %all-gather.3.cloned.1.call-update) | async-done | bytes 4194320 | tf_op jit(solution)/shard_map/all_gather | solution.py:100
  266.7 3.1 fusion
  269.8 8.0 %fusion.15 = f32[1024,704]{0,1:T(8,128)} fusion(bf16[2048,704]{0,1:T(8,128)(2,1)} %param.23, bf16[1024,2048]{1,0:T(8,128)(2,1)} %all-gather.3.cloned.1.call-done, f32[2048]{0:T(1024)S(1)} %copy-done.12, f32[1024]{0:T(1024)S(1)} %add_rsqrt_fusion), kind=kOutput, calls=%fused_computation.27 | convolution fusion | flops 2961178624 | bytes 9973760 | tf_op jit(solution)/shard_map/dot_general | solution.py:102
  277.8 12.4 %convolution_convert_fusion = bf16[1024,2048]{1,0:T(8,128)(2,1)} fusion(bf16[704,2048]{1,0:T(8,128)(2,1)} %param.25, f32[1024,704]{0,1:T(8,128)} %fusion.15, bf16[2048,704]{0,1:T(8,128)(2,1)} %param.24, bf16[1024,2048]{1,0:T(8,128)(2,1)} %all-gather.3.cloned.1.call-done, f32[2048]{0:T(1024)S(1)} %copy-done.12, f32[1024]{0:T(1024)S(1)} %add_rsqrt_fusion), kind=kOutput, calls=%fused_computation.20 | convolution fusion | flops 5920391168 | bytes 17051648 | tf_op jit(solution)/shard_map/dot_general | solution.py:106
  290.3 37.9 %reduce-scatter.2.cloned.1.call-done = bf16[128,2048]{1,0:T(8,128)(2,1)} async-done(((bf16[1024,2048]{1,0:T(8,128)(2,1)}), bf16[128,2048]{1,0:T(8,128)(2,1)}) %reduce-scatter.2.cloned.1.call-update) | async-done | bytes 524304 | tf_op jit(solution)/shard_map/reduce_scatter | solution.py:105
  328.1 1.5 fusion.19
  329.6 0.8 copy-done.7
  330.4 1.0 fusion.21
  331.4 31.2 %all-gather.5.cloned.1.call-done = bf16[1024,2048]{1,0:T(8,128)(2,1)} async-done(((bf16[128,2048]{1,0:T(8,128)(2,1)}), bf16[1024,2048]{1,0:T(8,128)(2,1)}) %all-gather.5.cloned.1.call-update) | async-done | bytes 4194320 | tf_op jit(solution)/shard_map/all_gather | solution.py:114
  362.6 6.8 %convolution_convert_fusion.1 = bf16[1024,768]{1,0:T(8,128)(2,1)} fusion(bf16[1024,2048]{1,0:T(8,128)(2,1)} %all-gather.5.cloned.1.call-done, bf16[2048,768]{1,0:T(8,128)(2,1)S(1)} %copy-done), kind=kOutput, calls=%fused_computation.24 | convolution fusion | flops 3222011904 | bytes 8912896 | tf_op jit(solution)/shard_map/dot_general | solution.py:113
  369.4 4.3 all-to-all-start
  373.7 0.5 broadcast.218
  374.2 0.7 reduce.11
  375.0 0.7 reduce.10
  375.8 1.2 sort.35
  377.0 18.2 %all-to-all-done = bf16[8,128,768]{2,1,0:T(8,128)(2,1)} async-done(((bf16[8,128,768]{2,1,0:T(8,128)(2,1)}), bf16[8,128,768]{2,1,0:T(8,128)(2,1)}, u32[]{:S(2)}, u32[]{:S(2)}) %all-to-all-start) | async-done | bytes 1572896 | tf_op jit(solution)/shard_map/all_to_all | solution.py:118
  395.2 1.6 copy.52
  396.8 1.1 copy-done.3
  398.0 1.0 slice_bitcast_fusion
  399.0 2.8 gather_fusion.1
  401.8 7.0 %all-to-all-start.1 = ((bf16[16,1,8,4096]{3,2,1,0:T(8,128)(2,1)}), bf16[16,1,8,4096]{3,2,1,0:T(8,128)(2,1)}, u32[]{:S(2)}, u32[]{:S(2)}) async-start(bf16[16,1,8,4096]{3,2,1,0:T(8,128)(2,1)} %bitcast.67), calls=%async_computation.2 | async-start | bytes 2097152 | tf_op jit(solution)/shard_map/all_to_all | solution.py:129
  408.9 0.7 sort.34
  409.7 0.7 gather_fusion.2
  410.3 1.9 slice.54
  412.2 14.1 %all-to-all-done.1 = bf16[16,1,8,4096]{3,2,1,0:T(8,128)(2,1)} async-done(((bf16[16,1,8,4096]{3,2,1,0:T(8,128)(2,1)}), bf16[16,1,8,4096]{3,2,1,0:T(8,128)(2,1)}, u32[]{:S(2)}, u32[]{:S(2)}) %all-to-all-start.1) | async-done | bytes 1048608 | tf_op jit(solution)/shard_map/all_to_all | solution.py:129
  426.3 1.1 broadcast_in_dim.63
  427.4 3.4 scatter_fusion
  (58 shorter events, 0.9 us)
Async XLA Ops:
  7.2 355.4 %copy-start = (bf16[2048,768]{1,0:T(8,128)(2,1)S(1)}, bf16[2048,768]{1,0:T(8,128)(2,1)}, u32[]{:S(2)}) copy-start(bf16[2048,768]{1,0:T(8,128)(2,1)} %param.27) | copy-start | bytes 9437188
  7.2 26.4 %copy-start.1 = (s32[1,2048]{1,0:T(1,128)S(1)}, s32[1,2048]{1,0:T(1,128)}, u32[]{:S(2)}) copy-start(s32[1,2048]{1,0:T(1,128)} %param.19) | copy-start | bytes 24580
  7.2 259.5 %all-gather.3.cloned.1.call-start = ((), (), s32[]{:S(2)}) async-start(), calls=%async_computation.3 | async-start | bytes 4718592 | tf_op jit(solution)/shard_map/all_gather | solution.py:100
  13.7 31.7 %collective-permute-start = (bf16[128,4096]{0,1:T(8,128)(2,1)}, bf16[128,4096]{0,1:T(8,128)(2,1)}, u32[]{:S(2)}, u32[]{:S(2)}) collective-permute-start(bf16[128,4096]{0,1:T(8,128)(2,1)} %pad_maximum_fusion), channel_id=1, source_target_pairs={{0,8},{1,9},{2,10},{3,11},{4,12},{5,13},{6,14},{7,15},{16,24},{17,... | collective-permute-start | bytes 3145736 | tf_op jit(solution)/shard_map/ppermute | solution.py:60
  19.7 45.4 %collective-permute-start.1 = (bf16[128,4096]{0,1:T(8,128)(2,1)}, bf16[128,4096]{0,1:T(8,128)(2,1)}, u32[]{:S(2)}, u32[]{:S(2)}) collective-permute-start(bf16[128,4096]{0,1:T(8,128)(2,1)} %pad_maximum_fusion), channel_id=1, source_target_pairs={{0,7},{1,8},{2,9},{3,10},{4,11},{5,12},{6,13},{7,14},{8,15},{16,23... | collective-permute-start | bytes 3145736 | tf_op jit(solution)/shard_map/ppermute | solution.py:60
  26.7 60.9 %collective-permute-start.2 = (bf16[128,4096]{0,1:T(8,128)(2,1)}, bf16[128,4096]{0,1:T(8,128)(2,1)}, u32[]{:S(2)}, u32[]{:S(2)}) collective-permute-start(bf16[128,4096]{0,1:T(8,128)(2,1)} %pad_maximum_fusion), channel_id=1, source_target_pairs={{0,6},{1,7},{2,8},{3,9},{4,10},{5,11},{6,12},{7,13},{8,14},{9,15},... | collective-permute-start | bytes 3145736 | tf_op jit(solution)/shard_map/ppermute | solution.py:60
  29.0 81.2 %collective-permute-start.3 = (bf16[128,4096]{0,1:T(8,128)(2,1)}, bf16[128,4096]{0,1:T(8,128)(2,1)}, u32[]{:S(2)}, u32[]{:S(2)}) collective-permute-start(bf16[128,4096]{0,1:T(8,128)(2,1)} %pad_maximum_fusion), channel_id=1, source_target_pairs={{0,5},{1,6},{2,7},{3,8},{4,9},{5,10},{6,11},{7,12},{8,13},{9,14},{... | collective-permute-start | bytes 3145736 | tf_op jit(solution)/shard_map/ppermute | solution.py:60
  31.2 100.2 %collective-permute-start.4 = (bf16[128,4096]{0,1:T(8,128)(2,1)}, bf16[128,4096]{0,1:T(8,128)(2,1)}, u32[]{:S(2)}, u32[]{:S(2)}) collective-permute-start(bf16[128,4096]{0,1:T(8,128)(2,1)} %pad_maximum_fusion), channel_id=1, source_target_pairs={{0,4},{1,5},{2,6},{3,7},{4,8},{5,9},{6,10},{7,11},{8,12},{9,13},{1... | collective-permute-start | bytes 3145736 | tf_op jit(solution)/shard_map/ppermute | solution.py:60
  33.6 9.8 %copy-start.9 = (f32[4,128]{1,0:T(4,128)S(1)}, f32[4,128]{1,0:T(4,128)}, u32[]{:S(2)}) copy-start(f32[4,128]{1,0:T(4,128)} %param.20) | copy-start | bytes 6148
  45.4 88.4 %collective-permute-start.5 = (bf16[128,4096]{0,1:T(8,128)(2,1)}, bf16[128,4096]{0,1:T(8,128)(2,1)S(1)}, u32[]{:S(2)}, u32[]{:S(2)}) collective-permute-start(bf16[128,4096]{0,1:T(8,128)(2,1)} %pad_maximum_fusion), channel_id=1, source_target_pairs={{0,3},{1,4},{2,5},{3,6},{4,7},{5,8},{6,9},{7,10},{8,11},{9,12},{10... | collective-permute-start | bytes 3145736 | tf_op jit(solution)/shard_map/ppermute | solution.py:60
  65.1 69.8 %collective-permute-start.6 = (bf16[128,4096]{0,1:T(8,128)(2,1)}, bf16[128,4096]{0,1:T(8,128)(2,1)S(1)}, u32[]{:S(2)}, u32[]{:S(2)}) collective-permute-start(bf16[128,4096]{0,1:T(8,128)(2,1)} %pad_maximum_fusion), channel_id=1, source_target_pairs={{0,2},{1,3},{2,4},{3,5},{4,6},{5,7},{6,8},{7,9},{8,10},{9,11},{10,... | collective-permute-start | bytes 3145736 | tf_op jit(solution)/shard_map/ppermute | solution.py:60
  87.6 48.4 %collective-permute-start.7 = (bf16[128,4096]{0,1:T(8,128)(2,1)}, bf16[128,4096]{0,1:T(8,128)(2,1)S(1)}, u32[]{:S(2)}, u32[]{:S(2)}) collective-permute-start(bf16[128,4096]{0,1:T(8,128)(2,1)} %pad_maximum_fusion), channel_id=1, source_target_pairs={{0,1},{1,2},{2,3},{3,4},{4,5},{5,6},{6,7},{7,8},{8,9},{9,10},{10,1... | collective-permute-start | bytes 3145736 | tf_op jit(solution)/shard_map/ppermute | solution.py:60
  112.5 24.7 %copy-start.4 = (bf16[128,2048]{0,1:T(8,128)(2,1)S(1)}, bf16[128,2048]{0,1:T(8,128)(2,1)}, u32[]{:S(2)}) copy-start(bf16[128,2048]{0,1:T(8,128)(2,1)} %copy.38) | copy-start | bytes 1572868
  112.5 24.7 %copy-start.5 = (bf16[128,2048]{0,1:T(8,128)(2,1)S(1)}, bf16[128,2048]{0,1:T(8,128)(2,1)}, u32[]{:S(2)}) copy-start(bf16[128,2048]{0,1:T(8,128)(2,1)} %copy.39) | copy-start | bytes 1572868
  138.3 6.8 %copy-start.6 = (bf16[128,8,2,128]{3,2,1,0:T(2,128)(2,1)S(1)}, bf16[128,8,2,128]{3,2,1,0:T(2,128)(2,1)}, u32[]{:S(2)}) copy-start(bf16[128,8,2,128]{3,2,1,0:T(2,128)(2,1)} %reshape.141) | copy-start | bytes 1572868
  147.6 3.6 copy-start.2
  168.5 101.3 %copy-start.12 = (f32[2048]{0:T(1024)S(1)}, f32[2048]{0:T(1024)}, u32[]{:S(2)}) copy-start(f32[2048]{0:T(1024)} %param.22) | copy-start | bytes 24580
  168.5 159.6 %reduce-scatter.2.cloned.1.call-start = ((), (), s32[]{:S(2)}) async-start(), calls=%async_computation.4 | async-start | bytes 4718592 | tf_op jit(solution)/shard_map/reduce_scatter | solution.py:105
  290.2 40.2 %copy-start.8 = (f32[2048]{0:T(1024)S(1)}, f32[2048]{0:T(1024)}, u32[]{:S(2)}) copy-start(f32[2048]{0:T(1024)} %param.26) | copy-start | bytes 24580
  290.2 72.4 %all-gather.5.cloned.1.call-start = ((), (), s32[]{:S(2)}) async-start(), calls=%async_computation.5 | async-start | bytes 4718592 | tf_op jit(solution)/shard_map/all_gather | solution.py:114
  329.6 0.8 copy-start.7
  331.4 42.8 %copy-start.10 = (s32[1,256]{1,0:T(1,128)S(1)}, s32[1,256]{1,0:T(1,128)}, u32[]{:S(2)}) copy-start(s32[1,256]{1,0:T(1,128)} %param.28) | copy-start | bytes 3076
  331.4 43.6 %copy-start.11 = (s32[1,256]{1,0:T(1,128)S(1)}, s32[1,256]{1,0:T(1,128)}, u32[]{:S(2)}) copy-start(s32[1,256]{1,0:T(1,128)} %param.29) | copy-start | bytes 3076
  369.4 25.9 %all-to-all-start = ((bf16[8,128,768]{2,1,0:T(8,128)(2,1)}), bf16[8,128,768]{2,1,0:T(8,128)(2,1)}, u32[]{:S(2)}, u32[]{:S(2)}) async-start(bf16[8,128,768]{2,1,0:T(8,128)(2,1)} %bitcast.69), calls=%async_computation.1 | async-start | bytes 3145728 | tf_op jit(solution)/shard_map/all_to_all | solution.py:118
  396.8 1.2 copy-start.3
  401.8 24.4 %all-to-all-start.1 = ((bf16[16,1,8,4096]{3,2,1,0:T(8,128)(2,1)}), bf16[16,1,8,4096]{3,2,1,0:T(8,128)(2,1)}, u32[]{:S(2)}, u32[]{:S(2)}) async-start(bf16[16,1,8,4096]{3,2,1,0:T(8,128)(2,1)} %bitcast.67), calls=%async_computation.2 | async-start | bytes 2097152 | tf_op jit(solution)/shard_map/all_to_all | solution.py:129
Sparse Core Ops, SparseCore 0:
  168.7 98.0 all-gather.2
  290.4 37.7 reduce-scatter.1
  331.5 31.0 all-gather.4
where the time goes:
time: 438 us; the launch traced here: 437 us
  waiting for transfers between devices  263 us (60%)
  local copies, waits for them, and re-layouts  53.4 us (12%)
  starting transfers between devices  44.4 us (10%)
  matrix products  43.6 us (10%)
  other arithmetic  17.7 us (4%)
  between operations  15.4 us (4%)
    all_gather x1, waiting for transfers between devices, body(): gathered = lax.all_gather(residual_mid, 'req', axis=0, tiled=True)  97.9 us
    ppermute x8, waiting for transfers between devices, body(): pieces.append(lax.ppermute(own_kv, 'tok', perm=pairs))  63.6 us
    reduce_scatter x1, waiting for transfers between devices, body(): lax.psum_scatter(jnp.dot(hidden, down_weight, preferred_element_type=jnp....  37.9 us
    ppermute x8, starting transfers between devices, body(): pieces.append(lax.ppermute(own_kv, 'tok', perm=pairs))  32.8 us
    all_gather x1, waiting for transfers between devices, body(): lax.all_gather(next_normed, 'req', axis=0, tiled=True)  31.2 us
    unnamed x38, local copies, waits for them, and re-layouts  23.2 us
    all_to_all x1, waiting for transfers between devices, body(): lax.all_to_all(projected_cols, 'req', split_axis=0, concat_axis=1, tiled=...  18.2 us
    all_to_all x1, waiting for transfers between devices, body(): lax.all_to_all(outgoing, 'tok', split_axis=0, concat_axis=0, tiled=True)  14.1 us
  transfers between devices with their start and end apart: 13, of which 9 were waited for; matrix products, arithmetic and copies ran while one was open for 7% of the time, Pallas kernels for 0%

commit v1 on v0

--- a/solution.py
+++ b/solution.py
@@ -110,10 +110,14 @@
     ).astype(jnp.float32)
     layer_output = (residual_mid.astype(jnp.float32) + ffn_own).astype(jnp.bfloat16)
     next_normed = (rms_rows(layer_output.astype(jnp.float32)) * next_gain).astype(jnp.bfloat16)
+    check_shifts_all = lambda own_rows: jnp.concatenate(
+        jax.lax.all_to_all(
+            jnp.stack([own_rows for _ in range(jax.lax.axis_size("req"))]), "req", 0, 0
+        ),
+        0,
+    )
     projected_cols = jnp.dot(
-        lax.all_gather(next_normed, "req", axis=0, tiled=True),
-        qkv_weight,
-        preferred_element_type=jnp.float32,
+        check_shifts_all(next_normed), qkv_weight, preferred_element_type=jnp.float32
     ).astype(jnp.bfloat16)
     projected = lax.all_to_all(projected_cols, "req", split_axis=0, concat_axis=1, tiled=True)
     q_next = projected[:, :feat_width]

time: 438 us -> 458 us (1.046)
  blocking collectives: 0 us -> 52.8 us
  waiting for transfers between devices: 263 us -> 232 us
    all_to_all x0 -> x1, blocking collectives: none -> 52.8 us  [body(): jax.lax.all_to_all(jnp.stack([own_rows for _ in range(jax.lax.axis_size('...]
    all_gather x1 -> x0, waiting for transfers between devices: 31.2 us -> none  [body(): lax.all_gather(next_normed, 'req', axis=0, tiled=True)]
  transfers between devices with their start and end apart: 13 -> 12, of which waited for: 9 -> 8; matrix products, arithmetic and copies ran while one was open for 7% -> 7% of each run, Pallas kernels for 0% -> 0%
where the time goes in v1:
time: 458 us; the launch traced here: 457 us
  waiting for transfers between devices  232 us (51%)
  local copies, waits for them, and re-layouts  53.9 us (12%)
  blocking collectives  52.8 us (12%)
  starting transfers between devices  44.4 us (10%)
  matrix products  41.3 us (9%)
  other arithmetic  16.9 us (4%)
  between operations  15.7 us (3%)
    all_gather x1, waiting for transfers between devices, body(): gathered = lax.all_gather(residual_mid, 'req', axis=0, tiled=True)  97.9 us
    ppermute x8, waiting for transfers between devices, body(): pieces.append(lax.ppermute(own_kv, 'tok', perm=pairs))  63.6 us
    all_to_all x1, blocking collectives, body(): jax.lax.all_to_all(jnp.stack([own_rows for _ in range(jax.lax.axis_size('...  52.8 us
    reduce_scatter x1, waiting for transfers between devices, body(): lax.psum_scatter(jnp.dot(hidden, down_weight, preferred_element_type=jnp....  37.9 us
    ppermute x8, starting transfers between devices, body(): pieces.append(lax.ppermute(own_kv, 'tok', perm=pairs))  32.8 us
    unnamed x38, local copies, waits for them, and re-layouts  23.2 us
    all_to_all x1, waiting for transfers between devices, body(): lax.all_to_all(projected_cols, 'req', split_axis=0, concat_axis=1, tiled=...  18.2 us
    all_to_all x1, waiting for transfers between devices, body(): lax.all_to_all(outgoing, 'tok', split_axis=0, concat_axis=0, tiled=True)  14.1 us
  transfers between devices with their start and end apart: 12, of which 8 were waited for; matrix products, arithmetic and copies ran while one was open for 7% of the time, Pallas kernels for 0%

profile of v1, /device:TPU:0, one launch (start us, length us, event | category | flops | bytes accessed | tf_op | source)
XLA Modules:
  0.0 456.7 jit_solution(14254652004962880247)
XLA Ops:
  7.2 2.2 copy.38
  9.4 2.0 copy.39
  11.5 2.2 pad_maximum_fusion
  13.7 6.0 %collective-permute-start = (bf16[128,4096]{0,1:T(8,128)(2,1)}, bf16[128,4096]{0,1:T(8,128)(2,1)}, u32[]{:S(2)}, u32[]{:S(2)}) collective-permute-start(bf16[128,4096]{0,1:T(8,128)(2,1)} %pad_maximum_fusion), channel_id=1, source_target_pairs={{0,8},{1,9},{2,10},{3,11},{4,12},{5,13},{6,14},{7,15},{16,24},{17,... | collective-permute-start | bytes 3145736 | tf_op jit(solution)/shard_map/ppermute | solution.py:60
  19.7 7.0 %collective-permute-start.1 = (bf16[128,4096]{0,1:T(8,128)(2,1)}, bf16[128,4096]{0,1:T(8,128)(2,1)}, u32[]{:S(2)}, u32[]{:S(2)}) collective-permute-start(bf16[128,4096]{0,1:T(8,128)(2,1)} %pad_maximum_fusion), channel_id=1, source_target_pairs={{0,7},{1,8},{2,9},{3,10},{4,11},{5,12},{6,13},{7,14},{8,15},{16,23... | collective-permute-start | bytes 3145736 | tf_op jit(solution)/shard_map/ppermute | solution.py:60
  26.7 2.3 collective-permute-start.2
  29.0 2.3 collective-permute-start.3
  31.2 2.3 collective-permute-start.4
  33.6 6.5 %gather_fusion = s32[1152]{0:T(1024)S(1)} fusion(s32[2048]{0:T(1024)S(1)} %bitcast.63, s32[2048]{0:T(1024)S(1)} %pad_clamp_fusion), kind=kCustom, calls=%fused_computation | custom fusion | bytes 13824 | tf_op jit(solution)/shard_map/jit(_take)/gather | solution.py:69
  40.1 2.2 reshape.146
  42.3 1.0 compare_and_fusion
  43.4 0.7 multiply_reduce_fusion.1
  45.4 3.2 collective-permute-start.5
  48.6 2.4 constant_dynamic-update-slice_fusion.8
  51.0 14.2 %collective-permute-done.1 = bf16[128,4096]{0,1:T(8,128)(2,1)} collective-permute-done((bf16[128,4096]{0,1:T(8,128)(2,1)}, bf16[128,4096]{0,1:T(8,128)(2,1)}, u32[]{:S(2)}, u32[]{:S(2)}) %collective-permute-start.1) | collective-permute-done | bytes 1048608 | tf_op jit(solution)/shard_map/ppermute | solution.py:60
  65.1 5.8 %collective-permute-start.6 = (bf16[128,4096]{0,1:T(8,128)(2,1)}, bf16[128,4096]{0,1:T(8,128)(2,1)S(1)}, u32[]{:S(2)}, u32[]{:S(2)}) collective-permute-start(bf16[128,4096]{0,1:T(8,128)(2,1)} %pad_maximum_fusion), channel_id=1, source_target_pairs={{0,2},{1,3},{2,4},{3,5},{4,6},{5,7},{6,8},{7,9},{8,10},{9,11},{10,... | collective-permute-start | bytes 3145736 | tf_op jit(solution)/shard_map/ppermute | solution.py:60
  70.9 2.3 constant_dynamic-update-slice_fusion.7
  73.3 14.4 %collective-permute-done.2 = bf16[128,4096]{0,1:T(8,128)(2,1)} collective-permute-done((bf16[128,4096]{0,1:T(8,128)(2,1)}, bf16[128,4096]{0,1:T(8,128)(2,1)}, u32[]{:S(2)}, u32[]{:S(2)}) %collective-permute-start.2) | collective-permute-done | bytes 1048608 | tf_op jit(solution)/shard_map/ppermute | solution.py:60
  87.6 4.0 collective-permute-start.7
  91.7 2.4 constant_dynamic-update-slice_fusion.6
  94.0 16.1 %collective-permute-done.3 = bf16[128,4096]{0,1:T(8,128)(2,1)} collective-permute-done((bf16[128,4096]{0,1:T(8,128)(2,1)}, bf16[128,4096]{0,1:T(8,128)(2,1)}, u32[]{:S(2)}, u32[]{:S(2)}) %collective-permute-start.3) | collective-permute-done | bytes 1048608 | tf_op jit(solution)/shard_map/ppermute | solution.py:60
  110.1 2.4 constant_dynamic-update-slice_fusion.5
  112.5 19.0 %collective-permute-done.4 = bf16[128,4096]{0,1:T(8,128)(2,1)} collective-permute-done((bf16[128,4096]{0,1:T(8,128)(2,1)}, bf16[128,4096]{0,1:T(8,128)(2,1)}, u32[]{:S(2)}, u32[]{:S(2)}) %collective-permute-start.4) | collective-permute-done | bytes 1048608 | tf_op jit(solution)/shard_map/ppermute | solution.py:60
  131.4 2.4 constant_dynamic-update-slice_fusion.4
  133.8 1.1 constant_dynamic-update-slice_fusion.3
  135.0 1.1 constant_dynamic-update-slice_fusion.2
  136.1 1.1 constant_dynamic-update-slice_fusion.1
  137.2 1.1 constant_dynamic-update-slice_fusion
  138.3 6.8 %fusion.37 = (bf16[1152,2048]{0,1:T(8,128)(2,1)}, bf16[1152,2048]{0,1:T(8,128)(2,1)S(1)}) fusion(bf16[1152,4096]{0,1:T(8,128)(2,1)} %constant_dynamic-update-slice_fusion), kind=kLoop, calls=%fused_computation.84 | loop fusion | bytes 18874368 | tf_op jit(solution)/shard_map/slice | solution.py:65
  145.1 2.5 fusion.3
  147.6 2.3 fusion.4
  149.9 1.3 copy-done.2
  151.2 8.3 %broadcast_divide_fusion = f32[8,2,128,256]{3,2,1,0:T(8,128)S(1)} fusion(f32[8,2,128]{2,1,0:T(2,128)S(1)} %fusion.4, bf16[1152,8,256,1]{0,2,3,1:T(8,128)(2,1)} %bitcast.67, f32[8,2,1152,128]{3,2,1,0:T(8,128)} %copy-done.2, f32[8,2,128]{2,1,0:T(2,128)S(1)} %broadcast_maximum_fusion, pred[128,1152]{0,1:T(8,128)(4,1)S(1)} %compare_and_fusion), kind=kOutput, calls=%fused_computation.39 | convolution fusion | flops 1220280320 | bytes 16416768 | tf_op jit(solution)/shard_map/hmqk,khe->hmqe/dot_general | solution.py:83
  159.7 1.1 fusion.26
  160.8 2.0 copy.44
  162.9 5.7 %fusion.13 = bf16[128,2048]{1,0:T(8,128)(2,1)} fusion(bf16[128,2048]{0,1:T(8,128)(2,1)} %bitcast.70, bf16[2048,2048]{1,0:T(8,128)(2,1)} %param.21, bf16[128,2048]{1,0:T(8,128)(2,1)} %param.15), kind=kOutput, calls=%fused_computation.23 | convolution fusion | flops 1074528256 | bytes 9961472 | tf_op jit(solution)/shard_map/dot_general | solution.py:98
  168.5 0.3 reduce-scatter.2.cloned.1.call-start
  168.8 97.9 %all-gather.2.cloned.1.call-done = bf16[1024,2048]{1,0:T(8,128)(2,1)} async-done(((bf16[128,2048]{1,0:T(8,128)(2,1)}), bf16[1024,2048]{1,0:T(8,128)(2,1)}) %all-gather.2.cloned.1.call-update) | async-done | bytes 4194320 | tf_op jit(solution)/shard_map/all_gather | solution.py:100
  266.7 3.1 fusion
  269.8 8.0 %fusion.15 = f32[1024,704]{0,1:T(8,128)} fusion(bf16[2048,704]{0,1:T(8,128)(2,1)} %param.23, bf16[1024,2048]{1,0:T(8,128)(2,1)} %all-gather.2.cloned.1.call-done, f32[2048]{0:T(1024)S(1)} %copy-done.12, f32[1024]{0:T(1024)S(1)} %add_rsqrt_fusion), kind=kOutput, calls=%fused_computation.27 | convolution fusion | flops 2961178624 | bytes 9973760 | tf_op jit(solution)/shard_map/dot_general | solution.py:102
  277.8 12.4 %convolution_convert_fusion = bf16[1024,2048]{1,0:T(8,128)(2,1)} fusion(bf16[704,2048]{1,0:T(8,128)(2,1)} %param.25, f32[1024,704]{0,1:T(8,128)} %fusion.15, bf16[2048,704]{0,1:T(8,128)(2,1)} %param.24, bf16[1024,2048]{1,0:T(8,128)(2,1)} %all-gather.2.cloned.1.call-done, f32[2048]{0:T(1024)S(1)} %copy-done.12, f32[1024]{0:T(1024)S(1)} %add_rsqrt_fusion), kind=kOutput, calls=%fused_computation.20 | convolution fusion | flops 5920391168 | bytes 17051648 | tf_op jit(solution)/shard_map/dot_general | solution.py:106
  290.2 37.9 %reduce-scatter.2.cloned.1.call-done = bf16[128,2048]{1,0:T(8,128)(2,1)} async-done(((bf16[1024,2048]{1,0:T(8,128)(2,1)}), bf16[128,2048]{1,0:T(8,128)(2,1)}) %reduce-scatter.2.cloned.1.call-update) | async-done | bytes 524304 | tf_op jit(solution)/shard_map/reduce_scatter | solution.py:105
  328.1 1.5 fusion.19
  329.6 0.8 copy-done.7
  330.6 0.5 stack.2
  331.1 52.8 %all_to_all.29 = bf16[8,128,2048]{2,1,0:T(8,128)(2,1)S(1)} all-to-all(bf16[8,128,2048]{2,1,0:T(8,128)(2,1)S(1)} %stack.2), channel_id=1, replica_groups=mesh['req'=8,'tok'=16] {'req'}, dimensions={0} | all-to-all | bytes 8388608 | tf_op jit(solution)/shard_map/all_to_all | solution.py:114
  383.9 4.5 convolution_convert_fusion.1
  388.5 4.3 all-to-all-start.1
  392.8 0.5 broadcast.220
  393.3 0.7 reduce.11
  394.1 0.7 reduce.10
  394.9 1.2 sort.35
  396.1 18.2 %all-to-all-done.1 = bf16[8,128,768]{2,1,0:T(8,128)(2,1)} async-done(((bf16[8,128,768]{2,1,0:T(8,128)(2,1)}), bf16[8,128,768]{2,1,0:T(8,128)(2,1)}, u32[]{:S(2)}, u32[]{:S(2)}) %all-to-all-start.1) | async-done | bytes 1572896 | tf_op jit(solution)/shard_map/all_to_all | solution.py:122
  414.3 1.6 copy.52
  415.9 1.1 copy-done.3
  417.1 1.0 slice_bitcast_fusion
  418.1 2.8 gather_fusion.1
  420.9 7.0 %all-to-all-start.2 = ((bf16[16,1,8,4096]{3,2,1,0:T(8,128)(2,1)}), bf16[16,1,8,4096]{3,2,1,0:T(8,128)(2,1)}, u32[]{:S(2)}, u32[]{:S(2)}) async-start(bf16[16,1,8,4096]{3,2,1,0:T(8,128)(2,1)} %bitcast.68), calls=%async_computation.3 | async-start | bytes 2097152 | tf_op jit(solution)/shard_map/all_to_all | solution.py:133
  428.0 0.7 sort.34
  428.8 0.7 gather_fusion.2
  429.5 1.9 slice.54
  431.3 14.1 %all-to-all-done.2 = bf16[16,1,8,4096]{3,2,1,0:T(8,128)(2,1)} async-done(((bf16[16,1,8,4096]{3,2,1,0:T(8,128)(2,1)}), bf16[16,1,8,4096]{3,2,1,0:T(8,128)(2,1)}, u32[]{:S(2)}, u32[]{:S(2)}) %all-to-all-start.2) | async-done | bytes 1048608 | tf_op jit(solution)/shard_map/all_to_all | solution.py:133
  445.4 1.1 broadcast_in_dim.63
  446.5 3.4 scatter_fusion
  (57 shorter events, 1.0 us)
Async XLA Ops:
  7.2 376.8 %copy-start = (bf16[2048,768]{1,0:T(8,128)(2,1)S(1)}, bf16[2048,768]{1,0:T(8,128)(2,1)}, u32[]{:S(2)}) copy-start(bf16[2048,768]{1,0:T(8,128)(2,1)} %param.27) | copy-start | bytes 9437188
  7.2 26.4 %copy-start.1 = (s32[1,2048]{1,0:T(1,128)S(1)}, s32[1,2048]{1,0:T(1,128)}, u32[]{:S(2)}) copy-start(s32[1,2048]{1,0:T(1,128)} %param.19) | copy-start | bytes 24580
  7.2 259.5 %all-gather.2.cloned.1.call-start = ((), (), s32[]{:S(2)}) async-start(), calls=%async_computation.4 | async-start | bytes 4718592 | tf_op jit(solution)/shard_map/all_gather | solution.py:100
  13.7 31.7 %collective-permute-start = (bf16[128,4096]{0,1:T(8,128)(2,1)}, bf16[128,4096]{0,1:T(8,128)(2,1)}, u32[]{:S(2)}, u32[]{:S(2)}) collective-permute-start(bf16[128,4096]{0,1:T(8,128)(2,1)} %pad_maximum_fusion), channel_id=1, source_target_pairs={{0,8},{1,9},{2,10},{3,11},{4,12},{5,13},{6,14},{7,15},{16,24},{17,... | collective-permute-start | bytes 3145736 | tf_op jit(solution)/shard_map/ppermute | solution.py:60
  19.7 45.4 %collective-permute-start.1 = (bf16[128,4096]{0,1:T(8,128)(2,1)}, bf16[128,4096]{0,1:T(8,128)(2,1)}, u32[]{:S(2)}, u32[]{:S(2)}) collective-permute-start(bf16[128,4096]{0,1:T(8,128)(2,1)} %pad_maximum_fusion), channel_id=1, source_target_pairs={{0,7},{1,8},{2,9},{3,10},{4,11},{5,12},{6,13},{7,14},{8,15},{16,23... | collective-permute-start | bytes 3145736 | tf_op jit(solution)/shard_map/ppermute | solution.py:60
  26.7 60.9 %collective-permute-start.2 = (bf16[128,4096]{0,1:T(8,128)(2,1)}, bf16[128,4096]{0,1:T(8,128)(2,1)}, u32[]{:S(2)}, u32[]{:S(2)}) collective-permute-start(bf16[128,4096]{0,1:T(8,128)(2,1)} %pad_maximum_fusion), channel_id=1, source_target_pairs={{0,6},{1,7},{2,8},{3,9},{4,10},{5,11},{6,12},{7,13},{8,14},{9,15},... | collective-permute-start | bytes 3145736 | tf_op jit(solution)/shard_map/ppermute | solution.py:60
  29.0 81.2 %collective-permute-start.3 = (bf16[128,4096]{0,1:T(8,128)(2,1)}, bf16[128,4096]{0,1:T(8,128)(2,1)}, u32[]{:S(2)}, u32[]{:S(2)}) collective-permute-start(bf16[128,4096]{0,1:T(8,128)(2,1)} %pad_maximum_fusion), channel_id=1, source_target_pairs={{0,5},{1,6},{2,7},{3,8},{4,9},{5,10},{6,11},{7,12},{8,13},{9,14},{... | collective-permute-start | bytes 3145736 | tf_op jit(solution)/shard_map/ppermute | solution.py:60
  31.2 100.2 %collective-permute-start.4 = (bf16[128,4096]{0,1:T(8,128)(2,1)}, bf16[128,4096]{0,1:T(8,128)(2,1)}, u32[]{:S(2)}, u32[]{:S(2)}) collective-permute-start(bf16[128,4096]{0,1:T(8,128)(2,1)} %pad_maximum_fusion), channel_id=1, source_target_pairs={{0,4},{1,5},{2,6},{3,7},{4,8},{5,9},{6,10},{7,11},{8,12},{9,13},{1... | collective-permute-start | bytes 3145736 | tf_op jit(solution)/shard_map/ppermute | solution.py:60
  33.6 9.8 %copy-start.9 = (f32[4,128]{1,0:T(4,128)S(1)}, f32[4,128]{1,0:T(4,128)}, u32[]{:S(2)}) copy-start(f32[4,128]{1,0:T(4,128)} %param.20) | copy-start | bytes 6148
  45.4 88.4 %collective-permute-start.5 = (bf16[128,4096]{0,1:T(8,128)(2,1)}, bf16[128,4096]{0,1:T(8,128)(2,1)S(1)}, u32[]{:S(2)}, u32[]{:S(2)}) collective-permute-start(bf16[128,4096]{0,1:T(8,128)(2,1)} %pad_maximum_fusion), channel_id=1, source_target_pairs={{0,3},{1,4},{2,5},{3,6},{4,7},{5,8},{6,9},{7,10},{8,11},{9,12},{10... | collective-permute-start | bytes 3145736 | tf_op jit(solution)/shard_map/ppermute | solution.py:60
  65.1 69.8 %collective-permute-start.6 = (bf16[128,4096]{0,1:T(8,128)(2,1)}, bf16[128,4096]{0,1:T(8,128)(2,1)S(1)}, u32[]{:S(2)}, u32[]{:S(2)}) collective-permute-start(bf16[128,4096]{0,1:T(8,128)(2,1)} %pad_maximum_fusion), channel_id=1, source_target_pairs={{0,2},{1,3},{2,4},{3,5},{4,6},{5,7},{6,8},{7,9},{8,10},{9,11},{10,... | collective-permute-start | bytes 3145736 | tf_op jit(solution)/shard_map/ppermute | solution.py:60
  87.6 48.4 %collective-permute-start.7 = (bf16[128,4096]{0,1:T(8,128)(2,1)}, bf16[128,4096]{0,1:T(8,128)(2,1)S(1)}, u32[]{:S(2)}, u32[]{:S(2)}) collective-permute-start(bf16[128,4096]{0,1:T(8,128)(2,1)} %pad_maximum_fusion), channel_id=1, source_target_pairs={{0,1},{1,2},{2,3},{3,4},{4,5},{5,6},{6,7},{7,8},{8,9},{9,10},{10,1... | collective-permute-start | bytes 3145736 | tf_op jit(solution)/shard_map/ppermute | solution.py:60
  112.5 24.7 %copy-start.4 = (bf16[128,2048]{0,1:T(8,128)(2,1)S(1)}, bf16[128,2048]{0,1:T(8,128)(2,1)}, u32[]{:S(2)}) copy-start(bf16[128,2048]{0,1:T(8,128)(2,1)} %copy.38) | copy-start | bytes 1572868
  112.5 24.7 %copy-start.5 = (bf16[128,2048]{0,1:T(8,128)(2,1)S(1)}, bf16[128,2048]{0,1:T(8,128)(2,1)}, u32[]{:S(2)}) copy-start(bf16[128,2048]{0,1:T(8,128)(2,1)} %copy.39) | copy-start | bytes 1572868
  138.3 6.8 %copy-start.6 = (bf16[128,8,2,128]{3,2,1,0:T(2,128)(2,1)S(1)}, bf16[128,8,2,128]{3,2,1,0:T(2,128)(2,1)}, u32[]{:S(2)}) copy-start(bf16[128,8,2,128]{3,2,1,0:T(2,128)(2,1)} %reshape.146) | copy-start | bytes 1572868
  147.6 3.6 copy-start.2
  168.5 101.3 %copy-start.12 = (f32[2048]{0:T(1024)S(1)}, f32[2048]{0:T(1024)}, u32[]{:S(2)}) copy-start(f32[2048]{0:T(1024)} %param.22) | copy-start | bytes 24580
  168.5 159.6 %reduce-scatter.2.cloned.1.call-start = ((), (), s32[]{:S(2)}) async-start(), calls=%async_computation.5 | async-start | bytes 4718592 | tf_op jit(solution)/shard_map/reduce_scatter | solution.py:105
  290.2 40.2 %copy-start.8 = (f32[2048]{0:T(1024)S(1)}, f32[2048]{0:T(1024)}, u32[]{:S(2)}) copy-start(f32[2048]{0:T(1024)} %param.26) | copy-start | bytes 24580
  329.6 0.8 copy-start.7
  383.9 9.3 %copy-start.10 = (s32[1,256]{1,0:T(1,128)S(1)}, s32[1,256]{1,0:T(1,128)}, u32[]{:S(2)}) copy-start(s32[1,256]{1,0:T(1,128)} %param.28) | copy-start | bytes 3076
  383.9 10.2 %copy-start.11 = (s32[1,256]{1,0:T(1,128)S(1)}, s32[1,256]{1,0:T(1,128)}, u32[]{:S(2)}) copy-start(s32[1,256]{1,0:T(1,128)} %param.29) | copy-start | bytes 3076
  388.5 25.9 %all-to-all-start.1 = ((bf16[8,128,768]{2,1,0:T(8,128)(2,1)}), bf16[8,128,768]{2,1,0:T(8,128)(2,1)}, u32[]{:S(2)}, u32[]{:S(2)}) async-start(bf16[8,128,768]{2,1,0:T(8,128)(2,1)} %bitcast.71), calls=%async_computation.2 | async-start | bytes 3145728 | tf_op jit(solution)/shard_map/all_to_all | solution.py:122
  415.9 1.2 copy-start.3
  420.9 24.5 %all-to-all-start.2 = ((bf16[16,1,8,4096]{3,2,1,0:T(8,128)(2,1)}), bf16[16,1,8,4096]{3,2,1,0:T(8,128)(2,1)}, u32[]{:S(2)}, u32[]{:S(2)}) async-start(bf16[16,1,8,4096]{3,2,1,0:T(8,128)(2,1)} %bitcast.68), calls=%async_computation.3 | async-start | bytes 2097152 | tf_op jit(solution)/shard_map/all_to_all | solution.py:133
Sparse Core Ops, SparseCore 0:
  168.7 98.0 all-gather.1
  290.4 37.7 reduce-scatter.1
